TPU v7x, 32 devices: a whole 2x2x4 slice. The times are simulated.
32 devices in a mesh: grp: 2 (over y), tgt: 4 (over z), src: 4 (over x, core).
Axes of the slice: x: 2, y: 2, z: 4, core: 2. Of those that a mesh axis runs over, the one named last changes fastest.
Arguments:
- target_rows: bfloat16 [2048, 4608], P(('grp', 'tgt', 'src')), parts along dimension 0, may hold values from -6 to 6
- target_pos: int32 [2048], P(('grp', 'tgt')), parts along dimension 0, may hold values from 0 to 255
- decoder_rows: bfloat16 [512, 4608], P(('grp', 'tgt', 'src')), parts along dimension 0, may hold values from -0.09375 to 0.09375
- source_pos: int32 [512], P('grp'), parts along dimension 0, may hold values from 0 to 255
- out_proj: bfloat16 [32, 4608, 128], P('src', 'tgt'), may hold values from -0.09375 to 0.09375
- value_proj: bfloat16 [16, 4608, 128], P('src'), may hold values from -1 to 1
- attention: bfloat16 [64, 256, 256], P(('grp', 'src'), 'tgt'), parts along dimension 0, may hold values from 0 to 1, as said below
- tile_pattern: int32 [8, 4], P('grp'), parts along dimension 0, may hold values from 0 to 1, as said below
Outputs:
- edges: bfloat16 [512, 1024], P(('grp', 'src'), 'tgt'), parts along dimension 0
There are 2 independent parts, one for each index of `grp`. A program takes and returns all parts, laid end to end along the dimension named above; an argument that names none is the same for every part. Nothing has to cross between parts.
Inputs may be any that keep to these rules, and one draw needn't show every extreme that they name: Each row attention[h, p, :] is a probability distribution over the keys 0 to p: zero beyond p, summing to one. tile_pattern[b, c] is 1 where the tile of edges between source block b and target block c is kept, else 0.
All inputs are finite; a program needn't handle non-finite values.
Results may differ from a plain program's by a relative error of at most 0.0057.
Values may be sent and summed in bfloat16 or wider, within the bound.
No kernel may reach another device: no remote copies, remote signals or barrier semaphores. Data moves between devices by JAX's collectives and lax.ppermute only.
A program may use at most 64 MiB of HBM per device.

v0:
```python
import jax
import jax.numpy as jnp
from jax import lax
from jax.sharding import PartitionSpec as P


def passed_along(value, axis, steps):
    count = lax.axis_size(axis)
    pairs = [(source, (source + steps) % count) for source in range(count)]
    return lax.ppermute(value, axis, pairs)


def shards(
    target_rows, target_pos, decoder_rows, source_pos, out_proj, value_proj, attention, tile_pattern
):
    blocks = lax.axis_size("tgt")
    column = lax.axis_index("tgt")
    src_lane = lax.axis_index("src")
    full_targets, full_sources = (
        lax.all_gather(target_rows, "src", axis=0, tiled=True),
        lax.all_gather(decoder_rows, "src", axis=0, tiled=True),
    )
    tgt_dev = full_targets.shape[0]
    src_dev = full_sources.shape[0]
    sub_rows = decoder_rows.shape[0]
    heads_here = out_proj.shape[0]
    head_dim = out_proj.shape[2]
    groups_here = value_proj.shape[0]
    repeat = heads_here // groups_here
    read_sum = jnp.einsum(
        "td,hde->the",
        full_targets,
        lax.all_gather(out_proj, "tgt", axis=1, tiled=True),
        preferred_element_type=jnp.float32,
    )
    head_reads = read_sum.astype(jnp.bfloat16).reshape(tgt_dev, groups_here, repeat, head_dim)
    values = jnp.einsum("sd,gde->sge", full_sources, value_proj, preferred_element_type=jnp.float32)
    values = values.astype(jnp.bfloat16).reshape(src_dev, groups_here * head_dim)
    attn_table = lax.all_gather(attention, "tgt", axis=1, tiled=True)
    target_attn = jnp.take(attn_table, target_pos, axis=1)
    keyed_attn = jnp.transpose(target_attn, (0, 2, 1))

    def edge_tile(payload, block_index):
        decoder_part, value_part = payload
        key_positions = lax.dynamic_slice_in_dim(source_pos, block_index * src_dev, src_dev)
        weights = jnp.take(keyed_attn, key_positions, axis=1).astype(jnp.float32)
        scores = jnp.einsum(
            "sgd,tgrd->grst",
            value_part.reshape(src_dev, groups_here, head_dim),
            head_reads,
            preferred_element_type=jnp.float32,
        )
        scores = scores.reshape(heads_here, src_dev, tgt_dev)
        mixed_term = jnp.sum(weights * scores, axis=0)
        own_positions = lax.dynamic_slice_in_dim(key_positions, src_lane * sub_rows, sub_rows)
        same_place = (own_positions[:, None] == target_pos[None, :]).astype(jnp.float32)
        direct = (
            jnp.einsum("sd,td->st", decoder_part, full_targets, preferred_element_type=jnp.float32)
            * same_place
        )
        own_rows = lax.dynamic_slice_in_dim(mixed_term, src_lane * sub_rows, sub_rows, 0)
        return lax.dynamic_update_slice_in_dim(
            mixed_term, own_rows + direct, src_lane * sub_rows, 0
        )

    def place_tile(partial_value, payload, block_index):
        kept_flag = tile_pattern[block_index, column]
        piece_tile = edge_tile(payload, block_index) * kept_flag.astype(jnp.float32)
        return lax.dynamic_update_slice_in_dim(partial_value, piece_tile, block_index * src_dev, 0)

    own_block = (decoder_rows, values)
    partial_value = jnp.zeros((blocks * src_dev, tgt_dev), jnp.float32)
    partial_value = place_tile(partial_value, own_block, column)

    def cycle_turn(turn_index, state_carry):
        forward_block, backward_block, running = state_carry
        forward_block = passed_along((forward_block[0], forward_block[1]), "tgt", 1)
        backward_block = passed_along((backward_block[0], backward_block[1]), "tgt", -1)
        running = place_tile(running, forward_block, (column - turn_index) % blocks)
        running = place_tile(running, backward_block, (column + turn_index) % blocks)
        return (forward_block, backward_block, running)

    forward_block, backward_block, partial_value = lax.fori_loop(
        1, blocks // 2, cycle_turn, (own_block, own_block, partial_value)
    )
    forward_block = passed_along((forward_block[0], forward_block[1]), "tgt", 1)
    partial_value = place_tile(partial_value, forward_block, (column - blocks // 2) % blocks)
    summed = lax.psum_scatter(partial_value, "src", scatter_dimension=0, tiled=True)
    return summed.astype(jnp.bfloat16)


def solution(mesh):
    return jax.shard_map(
        shards,
        mesh=mesh,
        in_specs=(
            P(("grp", "tgt", "src"), None),
            P(("grp", "tgt")),
            P(("grp", "tgt", "src"), None),
            P("grp"),
            P("src", "tgt", None),
            P("src", None, None),
            P(("grp", "src"), "tgt", None),
            P("grp", None),
        ),
        out_specs=P(("grp", "src"), "tgt"),
        check_vma=False,
    )
```

profile of v0, /device:TPU:0, one launch (start us, length us, event | category | flops | bytes accessed | tf_op | source)
XLA Modules:
  0.0 277.3 jit_solution(18094460157816442848)
XLA Ops:
  6.5 1.9 copy.26
  8.5 0.7 all-gather.6.cloned.1.call-update
  9.2 0.7 all-gather.8.cloned.1.call-update
  10.0 5.1 %collective-permute-start.3 = (bf16[16,4608]{1,0:T(8,128)(2,1)S(1)}, bf16[16,4608]{1,0:T(8,128)(2,1)S(1)}, u32[]{:S(2)}, u32[]{:S(2)}) collective-permute-start(bf16[16,4608]{1,0:T(8,128)(2,1)S(1)} %copy-done.2), channel_id=1, source_target_pairs={{0,12},{4,0},{8,4},{12,8},{1,13},{5,1},{9,5},{13,9},{2,14},{6,2},{... | collective-permute-start | bytes 442376 | tf_op jit(solution)/shard_map/while/body/eval_jaxpr/ppermute | solution.py:10
  15.1 7.5 %all_gather.15 = bf16[64,4608]{1,0:T(8,128)(2,1)S(1)} all-gather(bf16[16,4608]{1,0:T(8,128)(2,1)S(1)} %copy-done.2), channel_id=1, replica_groups=mesh['grp'=2,'tgt'=4,'src'=4] {'src'}, dimensions={0}, use_global_device_ids=true | all-gather | bytes 737280 | tf_op jit(solution)/shard_map/all_gather | solution.py:21
  22.6 3.3 %convolution_convert_fusion = bf16[64,4,128]{2,0,1:T(8,128)(2,1)S(1)} fusion(bf16[4,4608,128]{2,1,0:T(8,128)(2,1)} %param.15, bf16[64,4608]{1,0:T(8,128)(2,1)S(1)} %all_gather.15), kind=kOutput, calls=%fused_computation.8 | convolution fusion | flops 302022656 | bytes 5373952 | tf_op jit(solution)/shard_map/sd,gde->sge/dot_general | solution.py:37
  26.0 3.9 %collective-permute-start.2 = (bf16[64,512]{1,0:T(8,128)(2,1)S(1)}, bf16[64,512]{1,0:T(8,128)(2,1)S(1)}, u32[]{:S(2)}, u32[]{:S(2)}) collective-permute-start(bf16[64,512]{1,0:T(8,128)(2,1)S(1)} %copy_bitcast_fusion), channel_id=1, source_target_pairs={{0,12},{4,0},{8,4},{12,8},{1,13},{5,1},{9,5},{13,9},{2,14},{6,2},{... | collective-permute-start | bytes 196616 | tf_op jit(solution)/shard_map/while/body/eval_jaxpr/ppermute | solution.py:10
  30.1 0.7 fusion.26
  33.4 4.4 %collective-permute-done = bf16[64,512]{1,0:T(8,128)(2,1)S(1)} collective-permute-done((bf16[64,512]{1,0:T(8,128)(2,1)S(1)}, bf16[64,512]{1,0:T(8,128)(2,1)S(1)}, u32[]{:S(2)}, u32[]{:S(2)}) %collective-permute-start) | collective-permute-done | bytes 65568 | tf_op jit(solution)/shard_map/while/body/eval_jaxpr/ppermute | solution.py:10
  37.8 1.1 collective-permute-start.4
  39.0 5.8 %collective-permute-done.4 = bf16[64,512]{1,0:T(8,128)(2,1)S(1)} collective-permute-done((bf16[64,512]{1,0:T(8,128)(2,1)S(1)}, bf16[64,512]{1,0:T(8,128)(2,1)S(1)}, u32[]{:S(2)}, u32[]{:S(2)}) %collective-permute-start.4) | collective-permute-done | bytes 65568 | tf_op jit(solution)/shard_map/ppermute | solution.py:10
  44.9 2.0 gather_fusion
  46.9 0.9 select_bitcast_fusion
  47.8 1.3 copy.27
  49.1 0.6 gather_fusion.4
  49.7 0.6 gather_fusion.3
  50.3 0.6 gather_fusion.2
  50.9 0.6 gather_fusion.1
  51.5 17.4 %all-gather.6.cloned.1.call-done = bf16[256,4608]{1,0:T(8,128)(2,1)} async-done(((bf16[64,4608]{1,0:T(8,128)(2,1)}), bf16[256,4608]{1,0:T(8,128)(2,1)}) %all-gather.6.cloned.1.call-update) | async-done | bytes 2359312 | tf_op jit(solution)/shard_map/all_gather | solution.py:20
  68.9 168.4 %all-gather.8.cloned.1.call-done = bf16[8,4608,128]{2,1,0:T(8,128)(2,1)} async-done(((bf16[8,1152,128]{2,1,0:T(8,128)(2,1)}), bf16[8,4608,128]{2,1,0:T(8,128)(2,1)}) %all-gather.8.cloned.1.call-update) | async-done | bytes 9437200 | tf_op jit(solution)/shard_map/all_gather | solution.py:33
  237.2 7.0 %fusion.2 = bf16[256,8,128]{2,0,1:T(8,128)(2,1)S(1)} fusion(bf16[8,4608,128]{2,1,0:T(8,128)(2,1)} %all-gather.8.cloned.1.call-done, bf16[256,4608]{1,0:T(8,128)(2,1)} %all-gather.6.cloned.1.call-done), kind=kOutput, calls=%fused_computation.7 | convolution fusion | flops 2416181248 | bytes 12320768 | tf_op jit(solution)/shard_map/td,hde->the/dot_general | solution.py:30
  245.5 0.4 fusion.16
  245.9 0.4 fusion.17
  246.3 0.7 fusion.12
  247.1 0.7 fusion.10
  247.9 0.4 fusion.15
  248.3 0.7 fusion.8
  249.1 0.4 fusion.14
  249.5 0.7 fusion.6
  250.3 0.7 copy-done.1
  251.0 18.4 %reduce-scatter.2.cloned.1.call-done = f32[64,256]{1,0:T(8,128)} async-done(((f32[256,256]{1,0:T(8,128)}), f32[64,256]{1,0:T(8,128)}) %reduce-scatter.2.cloned.1.call-update) | async-done | bytes 65552 | tf_op jit(solution)/shard_map/reduce_scatter | solution.py:88
  269.3 1.5 convert_element_type.69
  (46 shorter events, 1.9 us)
Async XLA Ops:
  6.5 3.4 %copy-start.2 = (bf16[16,4608]{1,0:T(8,128)(2,1)S(1)}, bf16[16,4608]{1,0:T(8,128)(2,1)}, u32[]{:S(2)}) copy-start(bf16[16,4608]{1,0:T(8,128)(2,1)} %param.12) | copy-start | bytes 442372
  6.5 38.4 %all-gather.4.cloned.1.call-start = ((), (), s32[]{:S(2)}) async-start(), calls=%async_computation.1 | async-start | bytes 1310720 | tf_op jit(solution)/shard_map/all_gather | solution.py:39
  8.4 60.4 %all-gather.6.cloned.1.call-start = ((), (), s32[]{:S(2)}) async-start(), calls=%async_computation.2 | async-start | bytes 2949120 | tf_op jit(solution)/shard_map/all_gather | solution.py:20
  9.2 228.1 %all-gather.8.cloned.1.call-start = ((), (), s32[]{:S(2)}) async-start(), calls=%async_computation.3 | async-start | bytes 11796480 | tf_op jit(solution)/shard_map/all_gather | solution.py:33
  9.9 259.4 %reduce-scatter.2.cloned.1.call-start = ((), (), s32[]{:S(2)}) async-start(), calls=%async_computation.4 | async-start | bytes 327680 | tf_op jit(solution)/shard_map/reduce_scatter | solution.py:88
  10.0 238.3 %collective-permute-start.3 = (bf16[16,4608]{1,0:T(8,128)(2,1)S(1)}, bf16[16,4608]{1,0:T(8,128)(2,1)S(1)}, u32[]{:S(2)}, u32[]{:S(2)}) collective-permute-start(bf16[16,4608]{1,0:T(8,128)(2,1)S(1)} %copy-done.2), channel_id=1, source_target_pairs={{0,12},{4,0},{8,4},{12,8},{1,13},{5,1},{9,5},{13,9},{2,14},{6,2},{... | collective-permute-start | bytes 442376 | tf_op jit(solution)/shard_map/while/body/eval_jaxpr/ppermute | solution.py:10
  15.1 29.7 %collective-permute-start.1 = (bf16[16,4608]{1,0:T(8,128)(2,1)S(1)}, bf16[16,4608]{1,0:T(8,128)(2,1)S(1)}, u32[]{:S(2)}, u32[]{:S(2)}) collective-permute-start(bf16[16,4608]{1,0:T(8,128)(2,1)S(1)} %copy-done.2), channel_id=1, source_target_pairs={{0,4},{4,8},{8,12},{12,0},{1,5},{5,9},{9,13},{13,1},{2,6},{6,10},{... | collective-permute-start | bytes 442376 | tf_op jit(solution)/shard_map/while/body/eval_jaxpr/ppermute | solution.py:10
  22.6 7.2 %copy-start.3 = (s32[256]{0:T(256)S(1)}, s32[256]{0:T(256)}, u32[]{:S(2)}) copy-start(s32[256]{0:T(256)} %param.11) | copy-start | bytes 3076
  22.6 7.3 %copy-start.4 = (s32[256]{0:T(256)S(1)}, s32[256]{0:T(256)}, u32[]{:S(2)}) copy-start(s32[256]{0:T(256)} %param.13) | copy-start | bytes 3076
  22.6 7.5 %copy-start.5 = (s32[4,4]{1,0:T(4,128)S(1)}, s32[4,4]{1,0:T(4,128)}, u32[]{:S(2)}) copy-start(s32[4,4]{1,0:T(4,128)} %param.17) | copy-start | bytes 196
  26.0 13.0 %collective-permute-start.2 = (bf16[64,512]{1,0:T(8,128)(2,1)S(1)}, bf16[64,512]{1,0:T(8,128)(2,1)S(1)}, u32[]{:S(2)}, u32[]{:S(2)}) collective-permute-start(bf16[64,512]{1,0:T(8,128)(2,1)S(1)} %copy_bitcast_fusion), channel_id=1, source_target_pairs={{0,12},{4,0},{8,4},{12,8},{1,13},{5,1},{9,5},{13,9},{2,14},{6,2},{... | collective-permute-start | bytes 196616 | tf_op jit(solution)/shard_map/while/body/eval_jaxpr/ppermute | solution.py:10
  29.8 7.9 %collective-permute-start = (bf16[64,512]{1,0:T(8,128)(2,1)S(1)}, bf16[64,512]{1,0:T(8,128)(2,1)S(1)}, u32[]{:S(2)}, u32[]{:S(2)}) collective-permute-start(bf16[64,512]{1,0:T(8,128)(2,1)S(1)} %copy_bitcast_fusion), channel_id=1, source_target_pairs={{0,4},{4,8},{8,12},{12,0},{1,5},{5,9},{9,13},{13,1},{2,6},{6,10},{... | collective-permute-start | bytes 196616 | tf_op jit(solution)/shard_map/while/body/eval_jaxpr/ppermute | solution.py:10
  37.8 7.0 %collective-permute-start.4 = (bf16[64,512]{1,0:T(8,128)(2,1)S(1)}, bf16[64,512]{1,0:T(8,128)(2,1)S(1)}, u32[]{:S(2)}, u32[]{:S(2)}) collective-permute-start(bf16[64,512]{1,0:T(8,128)(2,1)S(1)} %collective-permute-done), channel_id=1, source_target_pairs={{0,4},{4,8},{8,12},{12,0},{1,5},{5,9},{9,13},{13,1},{2,6},{6,10},{... | collective-permute-start | bytes 196616 | tf_op jit(solution)/shard_map/ppermute | solution.py:10
  44.8 204.7 %collective-permute-start.5 = (bf16[16,4608]{1,0:T(8,128)(2,1)S(1)}, bf16[16,4608]{1,0:T(8,128)(2,1)S(1)}, u32[]{:S(2)}, u32[]{:S(2)}) collective-permute-start(bf16[16,4608]{1,0:T(8,128)(2,1)S(1)} %collective-permute-done.1), channel_id=1, source_target_pairs={{0,4},{4,8},{8,12},{12,0},{1,5},{5,9},{9,13},{13,1},{2,6},{6,10},{... | collective-permute-start | bytes 442376 | tf_op jit(solution)/shard_map/ppermute | solution.py:10
  244.5 1.8 copy-start
  250.3 0.7 copy-start.1
Sparse Core Ops, SparseCore 0:
  8.9 33.7 all-gather.3
  44.2 24.5 all-gather.5
  70.4 166.7 all-gather.7
  251.1 18.2 reduce-scatter.1
where the time goes:
time: 278 us; the launch traced here: 277 us
  waiting for transfers between devices  216 us (78%)
  between operations  16 us (6%)
  matrix products  14.3 us (5%)
  starting transfers between devices  10.4 us (4%)
  local copies, waits for them, and re-layouts  9.07 us (3%)
  blocking collectives  7.51 us (3%)
  other arithmetic  4.37 us (2%)
    all_gather x1, waiting for transfers between devices, shards(): lax.all_gather(out_proj, 'tgt', axis=1, tiled=True)  168 us
    reduce_scatter x1, waiting for transfers between devices, shards(): lax.psum_scatter(partial_value, 'src', scatter_dimension=0, tiled=True)  18.4 us
    all_gather x1, waiting for transfers between devices, shards(): lax.all_gather(target_rows, 'src', axis=0, tiled=True)  17.4 us
    ppermute x6, starting transfers between devices, passed_along(): return lax.ppermute(value, axis, pairs)  10.2 us
    ppermute x6, waiting for transfers between devices, passed_along(): return lax.ppermute(value, axis, pairs)  10.2 us
    all_gather x1, blocking collectives, shards(): lax.all_gather(decoder_rows, 'src', axis=0, tiled=True)  7.51 us
    dot_general x1, matrix products, shards(): jnp.einsum('td,hde->the', full_targets, lax.all_gather(out_proj, 'tgt', a...  6.99 us
  transfers between devices with their start and end apart: 10, of which 5 were waited for; matrix products, arithmetic and copies ran while one was open for 8% of the time, Pallas kernels for 0%

commit v1 on v0

--- a/solution.py
+++ b/solution.py
@@ -1,7 +1,15 @@
+import functools
+
 import jax
 import jax.numpy as jnp
 from jax import lax
+from jax.experimental import pallas as pl
+from jax.experimental.pallas import tpu as pltpu
 from jax.sharding import PartitionSpec as P
+
+F32 = jnp.float32
+BF16 = jnp.bfloat16
+VMEM_BYTES = 48 << 20
 
 
 def passed_along(value, axis, steps):
@@ -10,7 +18,303 @@
     return lax.ppermute(value, axis, pairs)
 
 
-def shards(
+def swapped(value, axis, bit):
+    pairs = [(source, source ^ bit) for source in range(lax.axis_size(axis))]
+    return lax.ppermute(value, axis, pairs)
+
+
+def kernel_call(body, outs, grid, in_specs, out_specs, scratch, scalars, args, flops, moved):
+    return pl.pallas_call(
+        body,
+        out_shape=outs,
+        grid_spec=pltpu.PrefetchScalarGridSpec(
+            num_scalar_prefetch=1,
+            grid=grid,
+            in_specs=in_specs,
+            out_specs=out_specs,
+            scratch_shapes=scratch,
+        ),
+        compiler_params=pltpu.CompilerParams(
+            dimension_semantics=("arbitrary",) * len(grid), vmem_limit_bytes=VMEM_BYTES
+        ),
+        cost_estimate=pl.CostEstimate(flops=flops, bytes_accessed=moved, transcendentals=0),
+    )(scalars, *args)
+
+
+def whole(array, rows=None):
+    shape = array.shape if rows is None else (rows,) + array.shape[1:]
+    return pl.BlockSpec(shape, lambda *_: (0,) * len(shape))
+
+
+def pair_of(ref, first):
+    return jnp.concatenate([ref[first], ref[first + 1]], axis=-1)
+
+
+def payload_kernel(rows, lane, own, core, far, cross, value, attn, spos, tpos, out, total):
+    step = pl.program_id(0)
+    subs = own.shape[0] - rows
+    sub = subs // pl.num_programs(0)
+    heads, queries, keys = attn.shape
+    groups = value.shape[0]
+    sources = spos.shape[1]
+    base = heads * queries
+    block = 4 * sub
+
+    @pl.when(step == 0)
+    def _():
+        total[...] = jnp.zeros_like(total)
+        picks = lax.broadcasted_iota(jnp.int32, (keys, sources), 0) == spos[...]
+        picks = picks.astype(F32).astype(BF16)
+        table = attn[...].reshape(base, keys)
+        out[0:base, :] = jnp.dot(table, picks, preferred_element_type=F32).astype(BF16)
+        tail = out.shape[0] - base - block * (groups // 2)
+        out[out.shape[0] - tail :, :] = jnp.broadcast_to(
+            tpos[...].astype(F32), (tail, tpos.shape[1])
+        ).astype(BF16)
+
+    at = pl.ds(pl.multiple_of(rows + step * sub, sub), sub)
+    left = jnp.concatenate([own[at, :], core[at, :], far[at, :], cross[at, :]], axis=0)
+    for pair in range(groups // 2):
+        cols = slice(pair * sources, (pair + 1) * sources)
+        total[:, cols] += jnp.dot(left, pair_of(value, 2 * pair), preferred_element_type=F32)
+
+    @pl.when(step == pl.num_programs(0) - 1)
+    def _():
+        for pair in range(groups // 2):
+            cols = slice(pair * sources, (pair + 1) * sources)
+            for j in range(4):
+                spot = pl.multiple_of(base + pair * block + lane[j] * sub, sub)
+                out[pl.ds(spot, sub), :] = total[j * sub : (j + 1) * sub, cols].astype(BF16)
+
+
+def reads_kernel(rows, info, own, core, far, cross, first, second, third, fourth, weight, reads, direct, dec):
+    sub = second.shape[0] - rows
+    dec[...] = jnp.zeros_like(dec)
+    for k, ref in enumerate((first, second, third, fourth)):
+        if k:
+            piece = ref[rows:, :]
+        else:
+            piece = ref[pl.ds(pl.multiple_of(info[8], sub), sub), :]
+        dec[pl.ds(pl.multiple_of(info[4 + k], sub), sub), :] = piece
+    left = jnp.concatenate([ref[0:rows, :] for ref in (own, core, far, cross)], axis=0)
+    width = 2 * weight.shape[2]
+
+    def put(target, cols, value):
+        for j in range(4):
+            spot = pl.multiple_of(info[j] * rows, rows)
+            target[pl.ds(spot, rows), cols] = value[j * rows : (j + 1) * rows].astype(target.dtype)
+
+    for pair in range(weight.shape[0] // 2):
+        got = jnp.dot(left, pair_of(weight, 2 * pair), preferred_element_type=F32)
+        put(reads, slice(pair * width, (pair + 1) * width), got)
+    put(
+        direct,
+        slice(0, direct.shape[1]),
+        lax.dot_general(left, dec[...], (((1,), (1,)), ((), ())), preferred_element_type=F32),
+    )
+
+
+def edges_kernel(heads, queries, info, *refs):
+    home, right1, right2, right3, left1, left2, left3 = refs[:7]
+    reads = refs[7:11]
+    direct = refs[11:15]
+    spos, out, table, values = refs[15:]
+    sources = spos.shape[1]
+    half = sources // 2
+    base = heads * queries
+    block = sources // 4
+    wide = 2 * (reads[0].shape[1] // heads)
+    dim = wide // 2
+    pairs = heads // 2
+    here = info[8]
+    table[0] = home[...]
+    for k, (near, other) in enumerate(((right1, left3), (right2, left2), (right3, left1)), 1):
+
+        @pl.when(here >= k)
+        def _(k=k, near=near):
+            table[k] = near[...]
+
+        @pl.when(here < k)
+        def _(k=k, other=other):
+            table[k] = other[...]
+
+    for k in range(4):
+        for p in range(pairs // 2):
+            values[pl.ds(pl.multiple_of(info[4 + k], block), block), p * sources : (p + 1) * sources] = (
+                table[k, base + p * block : base + (p + 1) * block, :]
+            )
+    lanes = pl.ds(pl.multiple_of(info[9] * half, half), half)
+    spot = pl.multiple_of(info[9] * half, half)
+    grid_q = jnp.concatenate(
+        [lax.broadcasted_iota(jnp.int32, (queries, sources), 0) + info[k] for k in range(4)], axis=0
+    )
+    picks = (grid_q[:, :half] == spos[:, lanes]).astype(F32).astype(BF16)
+    blank = jnp.zeros((dim, half), BF16)
+    scorers, tables = [], []
+    for pair in range(pairs):
+        turned = values[pl.ds(spot, half), pair * dim : (pair + 1) * dim].astype(F32).T.astype(BF16)
+        scorers.append(
+            jnp.concatenate(
+                [
+                    jnp.concatenate([turned, blank], axis=1),
+                    jnp.concatenate([blank, turned], axis=1),
+                ],
+                axis=0,
+            )
+        )
+        tables.append(
+            jnp.concatenate(
+                [
+                    jnp.concatenate(
+                        [table[k, h * queries : (h + 1) * queries, lanes] for k in range(4)], axis=0
+                    )
+                    for h in (2 * pair, 2 * pair + 1)
+                ],
+                axis=1,
+            )
+        )
+    for k in range(4):
+        tpos = table[k, table.shape[1] - 16 : table.shape[1], :].astype(F32)[0:1].astype(jnp.int32)
+        hot = (grid_q == tpos).astype(F32).T.astype(BF16)
+        running = None
+        for pair in range(pairs):
+            weights = jnp.dot(hot, tables[pair], preferred_element_type=F32)
+            scores = jnp.dot(
+                reads[k][:, pair * wide : (pair + 1) * wide], scorers[pair], preferred_element_type=F32
+            )
+            term = weights * scores
+            running = term if running is None else running + term
+        mixed = running[:, :half] + running[:, half:]
+        same = jnp.dot(hot, picks, preferred_element_type=F32)
+        turned = (mixed + same * direct[k][:, lanes]).T
+        cols = slice(k * sources, (k + 1) * sources)
+        for side in range(2):
+            row = pl.multiple_of(info[10 + side], block)
+            out[pl.ds(row, block), cols] = turned[side * block : (side + 1) * block, :]
+
+
+def resident(
+    target_rows, target_pos, decoder_rows, source_pos, out_proj, value_proj, attention, tile_pattern
+):
+    blocks = lax.axis_size("tgt")
+    z = lax.axis_index("tgt")
+    s = lax.axis_index("src")
+    rows, depth = target_rows.shape
+    sub = decoder_rows.shape[0]
+    part = depth // blocks
+    heads, _, head_dim = out_proj.shape
+    groups = value_proj.shape[0]
+    queries = attention.shape[1]
+    sources = source_pos.shape[0]
+    targets = target_pos.shape[0]
+    block = sources // blocks
+    ks = jnp.arange(4, dtype=jnp.int32)
+    lane = s ^ ks
+    origin = (z - ks) % blocks
+    source_spot = (origin % 2) * (2 * block) + (origin // 2) * block
+
+    stacked = [decoder_rows[:, i * part : (i + 1) * part] for i in range(blocks)]
+
+    def piece(array, column):
+        return lax.dynamic_slice_in_dim(array, column * part, part, 1)
+
+    outgoing = [
+        jnp.concatenate([piece(target_rows, (z + k) % blocks), piece(decoder_rows, (z + k) % blocks)], 0)
+        for k in range(1, blocks)
+    ]
+    own = [jnp.concatenate([piece(target_rows, z)] + stacked, 0)]
+    own += [passed_along(outgoing[k - 1], "tgt", k) for k in range(1, blocks)]
+    far = [swapped(value, "src", 2) for value in own]
+    core = [swapped(value, "src", 1) for value in own]
+    cross = [swapped(value, "src", 1) for value in far]
+
+    ordered = source_pos.reshape(2, 2, block).transpose(1, 0, 2).reshape(1, sources)
+    tall = heads * queries + block * (groups // 2) + 16
+    home = kernel_call(
+        functools.partial(payload_kernel, rows),
+        jax.ShapeDtypeStruct((tall, sources), BF16),
+        (blocks,),
+        [whole(own[0])] * 4
+        + [
+            pl.BlockSpec((groups, part, head_dim), lambda i, _: (0, i, 0)),
+            whole(attention),
+            whole(ordered),
+            pl.BlockSpec((1, targets), lambda *_: (0, 0)),
+        ],
+        pl.BlockSpec((tall, sources), lambda *_: (0, 0)),
+        [pltpu.VMEM((4 * sub, groups * head_dim), F32)],
+        lane,
+        [own[0], core[0], far[0], cross[0], value_proj, attention, ordered, target_pos[None, :]],
+        2 * 4 * sub * depth * groups * head_dim,
+        value_proj.size * 2,
+    )
+    rightward, leftward = [home], [home]
+    for step in range(1, blocks):
+        up = [(i, i + 1) for i in range(step - 1, blocks - 1)]
+        down = [(blocks - 1 - i, blocks - 2 - i) for i in range(step - 1, blocks - 1)]
+        rightward.append(lax.ppermute(rightward[-1], "tgt", up))
+        leftward.append(lax.ppermute(leftward[-1], "tgt", down))
+
+    info = jnp.concatenate([lane, source_spot + sub * s, (rows + sub * z)[None]]).astype(jnp.int32)
+    reads, direct = [], []
+    for k in range(blocks):
+        got = kernel_call(
+            functools.partial(reads_kernel, rows),
+            (
+                jax.ShapeDtypeStruct((4 * rows, heads * head_dim), BF16),
+                jax.ShapeDtypeStruct((4 * rows, sources), F32),
+            ),
+            (1,),
+            [whole(own[k], rows)] * 4 + [whole(a) for a in own] + [whole(out_proj)],
+            (
+                pl.BlockSpec((4 * rows, heads * head_dim), lambda *_: (0, 0)),
+                pl.BlockSpec((4 * rows, sources), lambda *_: (0, 0)),
+            ),
+            [pltpu.VMEM((sources, part), BF16)],
+            info,
+            [own[k], core[k], far[k], cross[k], *own, out_proj],
+            2 * 4 * rows * part * (heads * head_dim + sources),
+            out_proj.size * 2,
+        )
+        reads.append(got[0])
+        direct.append(got[1])
+
+    def edges(side):
+        x = s // 2
+        places = jnp.where(jnp.arange(2) == x, block, 0)
+        facts = jnp.concatenate([origin * queries, source_spot, z[None], side[None], places])
+        args = [home, *rightward[1:], *leftward[1:], *reads, *direct, ordered]
+        return kernel_call(
+            functools.partial(edges_kernel, heads, queries),
+            jax.ShapeDtypeStruct((sources // 2, blocks * targets), F32),
+            (1,),
+            [whole(a) for a in args],
+            pl.BlockSpec((sources // 2, blocks * targets), lambda *_: (0, 0)),
+            [
+                pltpu.VMEM((4,) + home.shape, BF16),
+                pltpu.VMEM((sources, groups * head_dim), BF16),
+            ],
+            facts.astype(jnp.int32),
+            args,
+            2 * 2 * blocks * targets * sources * heads * head_dim,
+            1 << 22,
+        )
+
+    side = s % 2
+    away = swapped(edges(1 - side), "src", 1)
+    kept = edges(side)
+    sent = (kept[:block] + away[:block]).astype(BF16)
+    back = swapped(sent, "src", 2)
+    mine = kept[block:] + away[block:] + back.astype(F32)
+    result = mine[:, :targets]
+    for k in range(1, blocks):
+        result = result + passed_along(
+            mine[:, k * targets : (k + 1) * targets].astype(BF16), "tgt", -k
+        ).astype(F32)
+    return (result * tile_pattern[s, z].astype(F32)).astype(BF16)
+
+
+def ring(
     target_rows, target_pos, decoder_rows, source_pos, out_proj, value_proj, attention, tile_pattern
 ):
     blocks = lax.axis_size("tgt")
@@ -87,6 +391,25 @@
     partial_value = place_tile(partial_value, forward_block, (column - blocks // 2) % blocks)
     summed = lax.psum_scatter(partial_value, "src", scatter_dimension=0, tiled=True)
     return summed.astype(jnp.bfloat16)
+
+
+def shards(*args):
+    target_rows, target_pos, decoder_rows, source_pos, out_proj, value_proj, attention, _ = args
+    blocks, lanes = lax.axis_size("tgt"), lax.axis_size("src")
+    heads, groups = out_proj.shape[0], value_proj.shape[0]
+    fits = (
+        blocks == 4
+        and lanes == 4
+        and out_proj.shape[1] % 128 == 0
+        and out_proj.shape[2] == 128
+        and heads == 2 * groups
+        and groups % 2 == 0
+        and source_pos.shape[0] == target_pos.shape[0] == attention.shape[2] == 256
+        and target_rows.shape[0] % 16 == 0
+        and decoder_rows.shape[0] % 16 == 0
+        and attention.shape[1] % 16 == 0
+    )
+    return resident(*args) if fits else ring(*args)
 
 
 def solution(mesh):

time: 278 us -> 106 us (0.38)
  waiting for transfers between devices: 216 us -> 20.8 us
  starting transfers between devices: 10.4 us -> 34.7 us
  Pallas kernels: 0 us -> 22.4 us
  between operations: 16 us -> 1.08 us
  matrix products: 14.3 us -> 0 us
  local copies, waits for them, and re-layouts: 9.07 us -> 19.3 us
  blocking collectives: 7.51 us -> 0 us
    all_gather x3 -> x0, waiting for transfers between devices: 186 us -> none  [the longest x1 168 us: shards(): lax.all_gather(out_proj, 'tgt', axis=1, tiled=True)]
    pallas_call x0 -> x7, Pallas kernels: none -> 22.4 us  [kernel_call(): pl.pallas_call(body, out_shape=outs, grid_spec=pltpu.PrefetchScalarGridSp...]
    ppermute x0 -> x20, starting transfers between devices: none -> 20.6 us  [the longest x14 8.7 us: swapped(): return lax.ppermute(value, axis, pairs)]
    reduce_scatter x1 -> x0, waiting for transfers between devices: 18.4 us -> none  [shards(): lax.psum_scatter(partial_value, 'src', scatter_dimension=0, tiled=True)]
    dot_general x10 -> x0, matrix products: 14.3 us -> none  [the longest x1 6.99 us: shards(): jnp.einsum('td,hde->the', full_targets, lax.all_gather(out_proj, 'tgt', a...]
    ppermute x0 -> x20, waiting for transfers between devices: none -> 13 us  [the longest x14 11.8 us: swapped(): return lax.ppermute(value, axis, pairs)]
    unnamed x13 -> x59, local copies, waits for them, and re-layouts: 2.56 us -> 13.6 us
    all_gather x1 -> x0, blocking collectives: 7.51 us -> none  [shards(): lax.all_gather(decoder_rows, 'src', axis=0, tiled=True)]
  transfers between devices with their start and end apart: 10 -> 26, of which waited for: 5 -> 8; matrix products, arithmetic and copies ran while one was open for 8% -> 7% of each run, Pallas kernels for 0% -> 18%
where the time goes in v1:
time: 106 us; the launch traced here: 105 us
  starting transfers between devices  34.7 us (33%)
  Pallas kernels  22.4 us (21%)
  waiting for transfers between devices  20.8 us (20%)
  local copies, waits for them, and re-layouts  19.3 us (18%)
  other arithmetic  6.54 us (6%)
  between operations  1.08 us (1%)
    pallas_call x7, Pallas kernels, kernel_call(): pl.pallas_call(body, out_shape=outs, grid_spec=pltpu.PrefetchScalarGridSp...  22.4 us
    ppermute x6, starting transfers between devices, passed_along(): return lax.ppermute(value, axis, pairs)  14.1 us
    unnamed x59, local copies, waits for them, and re-layouts  13.6 us
    ppermute x14, waiting for transfers between devices, swapped(): return lax.ppermute(value, axis, pairs)  11.8 us
    ppermute x14, starting transfers between devices, swapped(): return lax.ppermute(value, axis, pairs)  8.7 us
    ppermute x3, starting transfers between devices, resident(): rightward.append(lax.ppermute(rightward[-1], 'tgt', up))  8.09 us
    ppermute x6, waiting for transfers between devices, passed_along(): return lax.ppermute(value, axis, pairs)  7.84 us
    ppermute x3, starting transfers between devices, resident(): leftward.append(lax.ppermute(leftward[-1], 'tgt', down))  3.85 us
  transfers between devices with their start and end apart: 26, of which 8 were waited for; matrix products, arithmetic and copies ran while one was open for 7% of the time, Pallas kernels for 18%

profile of v1, /device:TPU:0, one launch (start us, length us, event | category | flops | bytes accessed | tf_op | source)
XLA Modules:
  0.0 104.9 jit_solution(2932932718417705247)
XLA Ops:
  0.0 1.3 %constant_dynamic-slice_fusion.1 = (bf16[64,1152]{1,0:T(8,128)(2,1)S(1)}, bf16[64,1152]{1,0:T(8,128)(2,1)S(1)}, bf16[128,1152]{1,0:T(8,128)(2,1)S(1)}, bf16[64,1152]{1,0:T(8,128)(2,1)S(1)}) fusion(bf16[64,4608]{1,0:T(8,128)(2,1)} %param.8, s32[]{:T(128)S(6)} %select_n.83, s32[]{:T(128)S(6)} %select_n.79, s32[]{:T(128)S(6)} %select_n.77, s32[]{:T(128)S(6)} %select_n.81), kind=kLoop, calls=%fused_computation.24 | loop fusion | bytes 1179664 | tf_op jit(solution)/shard_map/dynamic_slice | solution.py:219
  3.7 1.5 %constant_dynamic-slice_fusion = (bf16[16,1152]{1,0:T(8,128)(2,1)}, bf16[16,1152]{1,0:T(8,128)(2,1)S(1)}, bf16[128,1152]{1,0:T(8,128)(2,1)S(1)}, bf16[16,1152]{1,0:T(8,128)(2,1)S(1)}) fusion(bf16[16,4608]{1,0:T(8,128)(2,1)} %param.10, s32[]{:T(128)S(6)} %select_n.83, s32[]{:T(128)S(6)} %select_n.79, ...), kind=kLoop, calls=%fused_computation.23 | loop fusion | bytes 294924 | tf_op jit(solution)/shard_map/dynamic_slice | solution.py:219
  5.1 3.0 %collective-permute-start.1 = (bf16[128,1152]{1,0:T(8,128)(2,1)S(1)}, bf16[128,1152]{1,0:T(8,128)(2,1)S(1)}, u32[]{:S(2)}, u32[]{:S(2)}) collective-permute-start(bf16[128,1152]{1,0:T(8,128)(2,1)S(1)} %get-tuple-element.29.own.first), channel_id=1, source_target_pairs={{0,2},{1,3},{2,0},{3,1},{4,6},{5,7},{6,4},{7,5},{8,10},{9,11},{10,... | collective-permute-start | bytes 884744 | tf_op jit(solution)/shard_map/ppermute | solution.py:23
  8.8 2.6 %collective-permute-start.10 = (bf16[80,1152]{1,0:T(8,128)(2,1)}, bf16[80,1152]{1,0:T(8,128)(2,1)S(1)}, u32[]{:S(2)}, u32[]{:S(2)}) collective-permute-start(bf16[80,1152]{1,0:T(8,128)(2,1)} %pad_maximum_fusion.1), channel_id=1, source_target_pairs={{0,8},{4,12},{8,0},{12,4},{1,9},{5,13},{9,1},{13,5},{2,10},{6,14},... | collective-permute-start | bytes 552968 | tf_op jit(solution)/shard_map/ppermute | solution.py:18
  11.4 3.7 %collective-permute-done.1.far = bf16[128,1152]{1,0:T(8,128)(2,1)S(1)} collective-permute-done((bf16[128,1152]{1,0:T(8,128)(2,1)S(1)}, bf16[128,1152]{1,0:T(8,128)(2,1)S(1)}, u32[]{:S(2)}, u32[]{:S(2)}) %collective-permute-start.1) | collective-permute-done | bytes 294944 | tf_op jit(solution)/shard_map/ppermute | solution.py:23
  15.8 1.8 %collective-permute-start.9 = (bf16[80,1152]{1,0:T(8,128)(2,1)}, bf16[80,1152]{1,0:T(8,128)(2,1)S(1)}, u32[]{:S(2)}, u32[]{:S(2)}) collective-permute-start(bf16[80,1152]{1,0:T(8,128)(2,1)} %pad_maximum_fusion), channel_id=1, source_target_pairs={{0,4},{4,8},{8,12},{12,0},{1,5},{5,9},{9,13},{13,1},{2,6},{6,10},{... | collective-permute-start | bytes 552968 | tf_op jit(solution)/shard_map/ppermute | solution.py:18
  21.1 4.6 %shard_map.82.refs_0_ = bf16[656,256]{1,0:T(8,128)(2,1)S(1)} custom-call(s32[4]{0:T(128)S(1)} %iota_xor_fusion.lane, bf16[128,1152]{1,0:T(8,128)(2,1)S(1)} %get-tuple-element.29.own.first, bf16[128,1152]{1,0:T(8,128)(2,1)} %collective-permute-done.core, bf16[128,1152]{1,0:T(8,128)(2,1)S(1)} %copy-done.10, bf16[128,1152]{1,0:T(8,128)(2,1)} %collective-permute-done.2.cross, ...), custom_call_target="tpu_custom_call" | custom-call | flops 301989888 | bytes 4718592 | tf_op jit(solution)/shard_map/pallas_call | solution.py:27
  25.8 1.3 %collective-permute-start.6 = (bf16[656,256]{1,0:T(8,128)(2,1)S(1)}, bf16[656,256]{1,0:T(8,128)(2,1)}, u32[]{:S(2)}, u32[]{:S(2)}) collective-permute-start(bf16[656,256]{1,0:T(8,128)(2,1)S(1)} %shard_map.82.refs_0_), channel_id=1, source_target_pairs={{12,8},{8,4},{4,0},{13,9},{9,5},{5,1},{14,10},{10,6},{6,2},{15,11}... | collective-permute-start | bytes 1007624 | tf_op jit(solution)/shard_map/ppermute | solution.py:256
  27.1 5.3 %collective-permute-start.3 = (bf16[656,256]{1,0:T(8,128)(2,1)S(1)}, bf16[656,256]{1,0:T(8,128)(2,1)}, u32[]{:S(2)}, u32[]{:S(2)}) collective-permute-start(bf16[656,256]{1,0:T(8,128)(2,1)S(1)} %shard_map.82.refs_0_), channel_id=1, source_target_pairs={{0,4},{4,8},{8,12},{1,5},{5,9},{9,13},{2,6},{6,10},{10,14},{3,7},{... | collective-permute-start | bytes 1007624 | tf_op jit(solution)/shard_map/ppermute | solution.py:255
  32.4 1.4 %collective-permute-start.11 = (bf16[80,1152]{1,0:T(8,128)(2,1)S(1)}, bf16[80,1152]{1,0:T(8,128)(2,1)S(1)}, u32[]{:S(2)}, u32[]{:S(2)}) collective-permute-start(bf16[80,1152]{1,0:T(8,128)(2,1)S(1)} %pad_maximum_fusion.2), channel_id=1, source_target_pairs={{0,12},{4,0},{8,4},{12,8},{1,13},{5,1},{9,5},{13,9},{2,14},{6,2},{... | collective-permute-start | bytes 552968 | tf_op jit(solution)/shard_map/ppermute | solution.py:18
  33.8 1.5 %collective-permute-start.16 = (bf16[80,1152]{1,0:T(8,128)(2,1)S(1)}, bf16[80,1152]{1,0:T(8,128)(2,1)}, u32[]{:S(2)}, u32[]{:S(2)}) collective-permute-start(bf16[80,1152]{1,0:T(8,128)(2,1)S(1)} %collective-permute-done.10.third.own), channel_id=1, source_target_pairs={{0,2},{1,3},{2,0},{3,1},{4,6},{5,7},{6,4},{7,5},{8,10},{9,11},{10,... | collective-permute-start | bytes 552968 | tf_op jit(solution)/shard_map/ppermute | solution.py:23
  35.3 7.5 %collective-permute-done.11.fourth.own = bf16[80,1152]{1,0:T(8,128)(2,1)S(1)} collective-permute-done((bf16[80,1152]{1,0:T(8,128)(2,1)S(1)}, bf16[80,1152]{1,0:T(8,128)(2,1)S(1)}, u32[]{:S(2)}, u32[]{:S(2)}) %collective-permute-start.11) | collective-permute-done | bytes 184352 | tf_op jit(solution)/shard_map/ppermute | solution.py:18
  42.8 1.5 %collective-permute-start.19 = (bf16[80,1152]{1,0:T(8,128)(2,1)S(1)}, bf16[80,1152]{1,0:T(8,128)(2,1)}, u32[]{:S(2)}, u32[]{:S(2)}) collective-permute-start(bf16[80,1152]{1,0:T(8,128)(2,1)S(1)} %collective-permute-done.11.fourth.own), channel_id=1, source_target_pairs={{0,2},{1,3},{2,0},{3,1},{4,6},{5,7},{6,4},{7,5},{8,10},{9,11},{10,... | collective-permute-start | bytes 552968 | tf_op jit(solution)/shard_map/ppermute | solution.py:23
  44.9 1.3 %collective-permute-start.7 = (bf16[656,256]{1,0:T(8,128)(2,1)}, bf16[656,256]{1,0:T(8,128)(2,1)}, u32[]{:S(2)}, u32[]{:S(2)}) collective-permute-start(bf16[656,256]{1,0:T(8,128)(2,1)} %collective-permute-done.6.refs_4_), channel_id=1, source_target_pairs={{8,4},{4,0},{9,5},{5,1},{10,6},{6,2},{11,7},{7,3},{24,20},{20,16},... | collective-permute-start | bytes 1007624 | tf_op jit(solution)/shard_map/ppermute | solution.py:256
  46.2 1.4 %collective-permute-start.4 = (bf16[656,256]{1,0:T(8,128)(2,1)}, bf16[656,256]{1,0:T(8,128)(2,1)}, u32[]{:S(2)}, u32[]{:S(2)}) collective-permute-start(bf16[656,256]{1,0:T(8,128)(2,1)} %collective-permute-done.3.refs_1_), channel_id=1, source_target_pairs={{4,8},{8,12},{5,9},{9,13},{6,10},{10,14},{7,11},{11,15},{20,24},{2... | collective-permute-start | bytes 1007624 | tf_op jit(solution)/shard_map/ppermute | solution.py:255
  48.2 2.3 %collective-permute-done.19.far = bf16[80,1152]{1,0:T(8,128)(2,1)} collective-permute-done((bf16[80,1152]{1,0:T(8,128)(2,1)S(1)}, bf16[80,1152]{1,0:T(8,128)(2,1)}, u32[]{:S(2)}, u32[]{:S(2)}) %collective-permute-start.19) | collective-permute-done | bytes 184352 | tf_op jit(solution)/shard_map/ppermute | solution.py:23
  51.0 1.4 %collective-permute-done.13.far = bf16[80,1152]{1,0:T(8,128)(2,1)S(1)} collective-permute-done((bf16[80,1152]{1,0:T(8,128)(2,1)S(1)}, bf16[80,1152]{1,0:T(8,128)(2,1)S(1)}, u32[]{:S(2)}, u32[]{:S(2)}) %collective-permute-start.13) | collective-permute-done | bytes 184352 | tf_op jit(solution)/shard_map/ppermute | solution.py:23
  54.2 1.1 %collective-permute-done.7.refs_5_ = bf16[656,256]{1,0:T(8,128)(2,1)} collective-permute-done((bf16[656,256]{1,0:T(8,128)(2,1)}, bf16[656,256]{1,0:T(8,128)(2,1)}, u32[]{:S(2)}, u32[]{:S(2)}) %collective-permute-start.7) | collective-permute-done | bytes 335904 | tf_op jit(solution)/shard_map/ppermute | solution.py:256
  55.3 1.3 %collective-permute-start.8 = (bf16[656,256]{1,0:T(8,128)(2,1)}, bf16[656,256]{1,0:T(8,128)(2,1)}, u32[]{:S(2)}, u32[]{:S(2)}) collective-permute-start(bf16[656,256]{1,0:T(8,128)(2,1)} %collective-permute-done.7.refs_5_), channel_id=1, source_target_pairs={{4,0},{5,1},{6,2},{7,3},{20,16},{21,17},{22,18},{23,19}} | collective-permute-start | bytes 1007624 | tf_op jit(solution)/shard_map/ppermute | solution.py:256
  56.6 1.4 %collective-permute-start.5 = (bf16[656,256]{1,0:T(8,128)(2,1)}, bf16[656,256]{1,0:T(8,128)(2,1)}, u32[]{:S(2)}, u32[]{:S(2)}) collective-permute-start(bf16[656,256]{1,0:T(8,128)(2,1)} %collective-permute-done.4.refs_2_), channel_id=1, source_target_pairs={{8,12},{9,13},{10,14},{11,15},{24,28},{25,29},{26,30},{27,31}} | collective-permute-start | bytes 1007624 | tf_op jit(solution)/shard_map/ppermute | solution.py:255
  59.5 2.6 %shard_map.86 = (bf16[256,1024]{1,0:T(8,128)(2,1)S(1)}, f32[256,256]{1,0:T(8,128)S(1)}) custom-call(s32[9]{0:T(128)S(1)} %pad_add_fusion.info, bf16[80,1152]{1,0:T(8,128)(2,1)S(1)} %collective-permute-done.11.fourth.own, bf16[80,1152]{1,0:T(8,128)(2,1)} %collective-permute-done.18.core, bf16[80,1152]{1,0:T(8,128)(2,1)} %collective-permute-done.19.far, ...), custom_call_target="tpu_custom_call" | custom-call | flops 754974720 | bytes 2359296 | tf_op jit(solution)/shard_map/pallas_call | solution.py:27
  62.2 2.6 %shard_map.85 = (bf16[256,1024]{1,0:T(8,128)(2,1)S(1)}, f32[256,256]{1,0:T(8,128)S(1)}) custom-call(s32[9]{0:T(128)S(1)} %pad_add_fusion.info, bf16[80,1152]{1,0:T(8,128)(2,1)S(1)} %collective-permute-done.10.third.own, bf16[80,1152]{1,0:T(8,128)(2,1)} %collective-permute-done.15.core, bf16[80,1152]{1,0:T(8,128)(2,1)} %collective-permute-done.16.far, ...), custom_call_target="tpu_custom_call" | custom-call | flops 754974720 | bytes 2359296 | tf_op jit(solution)/shard_map/pallas_call | solution.py:27
  64.9 2.5 %shard_map.84 = (bf16[256,1024]{1,0:T(8,128)(2,1)S(1)}, f32[256,256]{1,0:T(8,128)S(1)}) custom-call(s32[9]{0:T(128)S(1)} %pad_add_fusion.info, bf16[80,1152]{1,0:T(8,128)(2,1)S(1)} %collective-permute-done.9.second.own, bf16[80,1152]{1,0:T(8,128)(2,1)} %collective-permute-done.12.core, bf16[80,1152]{1,0:T(8,128)(2,1)S(1)} %copy-done.22, ...), custom_call_target="tpu_custom_call" | custom-call | flops 754974720 | bytes 2359296 | tf_op jit(solution)/shard_map/pallas_call | solution.py:27
  67.5 2.5 %shard_map.83 = (bf16[256,1024]{1,0:T(8,128)(2,1)S(1)}, f32[256,256]{1,0:T(8,128)S(1)}) custom-call(s32[9]{0:T(128)S(1)} %pad_add_fusion.info, bf16[128,1152]{1,0:T(8,128)(2,1)S(1)} %get-tuple-element.29.own.first, bf16[128,1152]{1,0:T(8,128)(2,1)} %collective-permute-done.core, bf16[128,1152]{1,0:T(8,128)(2,1)S(1)} %copy-done.11, ...), custom_call_target="tpu_custom_call" | custom-call | flops 754974720 | bytes 2359296 | tf_op jit(solution)/shard_map/pallas_call | solution.py:27
  70.2 3.7 %shard_map.88 = f32[128,1024]{1,0:T(8,128)S(1)} custom-call(s32[12]{0:T(128)S(1)} %concatenate.27.info, bf16[656,256]{1,0:T(8,128)(2,1)S(1)} %shard_map.82.refs_0_, bf16[656,256]{1,0:T(8,128)(2,1)} %collective-permute-done.3.refs_1_, bf16[656,256]{1,0:T(8,128)(2,1)} %collective-permute-done.4.refs_2_, bf16[656,256]{1,0:T(8,128)(2,1)} %collective-permute-done.5.refs_3_, ...), custom_call_target="tpu_custom_call" | custom-call | flops 1073741824 | bytes 4194304 | tf_op jit(solution)/shard_map/pallas_call | solution.py:27
  74.1 1.0 copy-done.2
  82.1 3.7 %shard_map.87 = f32[128,1024]{1,0:T(8,128)S(1)} custom-call(s32[12]{0:T(128)S(1)} %concatenate.21.info, bf16[656,256]{1,0:T(8,128)(2,1)S(1)} %shard_map.82.refs_0_, bf16[656,256]{1,0:T(8,128)(2,1)} %collective-permute-done.3.refs_1_, bf16[656,256]{1,0:T(8,128)(2,1)} %collective-permute-done.4.refs_2_, bf16[656,256]{1,0:T(8,128)(2,1)} %collective-permute-done.5.refs_3_, ...), custom_call_target="tpu_custom_call" | custom-call | flops 1073741824 | bytes 4194304 | tf_op jit(solution)/shard_map/pallas_call | solution.py:27
  86.8 1.6 %collective-permute-start.22 = (bf16[64,1024]{1,0:T(8,128)(2,1)S(1)}, bf16[64,1024]{1,0:T(8,128)(2,1)S(1)}, u32[]{:S(2)}, u32[]{:S(2)}) collective-permute-start(bf16[64,1024]{1,0:T(8,128)(2,1)S(1)} %fusion), channel_id=1, source_target_pairs={{0,2},{1,3},{2,0},{3,1},{4,6},{5,7},{6,4},{7,5},{8,10},{9,11},{10,... | collective-permute-start | bytes 393224 | tf_op jit(solution)/shard_map/ppermute | solution.py:23
  88.3 4.4 %collective-permute-done.22 = bf16[64,1024]{1,0:T(8,128)(2,1)S(1)} collective-permute-done((bf16[64,1024]{1,0:T(8,128)(2,1)S(1)}, bf16[64,1024]{1,0:T(8,128)(2,1)S(1)}, u32[]{:S(2)}, u32[]{:S(2)}) %collective-permute-start.22) | collective-permute-done | bytes 131104 | tf_op jit(solution)/shard_map/ppermute | solution.py:23
  93.7 4.3 %collective-permute-start.23 = (bf16[64,256]{1,0:T(8,128)(2,1)S(1)}, bf16[64,256]{1,0:T(8,128)(2,1)S(1)}, u32[]{:S(2)}, u32[]{:S(2)}) collective-permute-start(bf16[64,256]{1,0:T(8,128)(2,1)S(1)} %get-tuple-element.31), channel_id=1, source_target_pairs={{0,12},{4,0},{8,4},{12,8},{1,13},{5,1},{9,5},{13,9},{2,14},{6,2},{... | collective-permute-start | bytes 98312 | tf_op jit(solution)/shard_map/ppermute | solution.py:18
  98.1 3.9 %collective-permute-start.24 = (bf16[64,256]{1,0:T(8,128)(2,1)S(1)}, bf16[64,256]{1,0:T(8,128)(2,1)S(1)}, u32[]{:S(2)}, u32[]{:S(2)}) collective-permute-start(bf16[64,256]{1,0:T(8,128)(2,1)S(1)} %get-tuple-element.33), channel_id=1, source_target_pairs={{0,8},{4,12},{8,0},{12,4},{1,9},{5,13},{9,1},{13,5},{2,10},{6,14},... | collective-permute-start | bytes 98312 | tf_op jit(solution)/shard_map/ppermute | solution.py:18
  102.0 1.3 %dynamic_slice.31 = s32[1,1]{1,0:T(1,128)} dynamic-slice(s32[4,4]{1,0:T(4,128)} %param.15, s32[]{:T(128)S(6)} %select_n.84, s32[]{:T(128)S(6)} %select_n.85), dynamic_slice_sizes={1,1} | dynamic-slice | bytes 12 | tf_op jit(solution)/shard_map/dynamic_slice | solution.py:314
  (106 shorter events, 22.4 us)
Async XLA Ops:
  0.0 59.5 %copy-start = (bf16[8,1152,128]{2,1,0:T(8,128)(2,1)S(1)}, bf16[8,1152,128]{2,1,0:T(8,128)(2,1)}, u32[]{:S(2)}) copy-start(bf16[8,1152,128]{2,1,0:T(8,128)(2,1)} %weight.7) | copy-start | bytes 7077892
  5.1 10.0 %collective-permute-start.1 = (bf16[128,1152]{1,0:T(8,128)(2,1)S(1)}, bf16[128,1152]{1,0:T(8,128)(2,1)S(1)}, u32[]{:S(2)}, u32[]{:S(2)}) collective-permute-start(bf16[128,1152]{1,0:T(8,128)(2,1)S(1)} %get-tuple-element.29.own.first), channel_id=1, source_target_pairs={{0,2},{1,3},{2,0},{3,1},{4,6},{5,7},{6,4},{7,5},{8,10},{9,11},{10,... | collective-permute-start | bytes 884744 | tf_op jit(solution)/shard_map/ppermute | solution.py:23
  8.1 10.4 %collective-permute-start = (bf16[128,1152]{1,0:T(8,128)(2,1)S(1)}, bf16[128,1152]{1,0:T(8,128)(2,1)}, u32[]{:S(2)}, u32[]{:S(2)}) collective-permute-start(bf16[128,1152]{1,0:T(8,128)(2,1)S(1)} %get-tuple-element.29.own.first), channel_id=1, source_target_pairs={{0,1},{1,0},{2,3},{3,2},{4,5},{5,4},{6,7},{7,6},{8,9},{9,8},{10,11... | collective-permute-start | bytes 884744 | tf_op jit(solution)/shard_map/ppermute | solution.py:23
  8.8 25.0 %collective-permute-start.10 = (bf16[80,1152]{1,0:T(8,128)(2,1)}, bf16[80,1152]{1,0:T(8,128)(2,1)S(1)}, u32[]{:S(2)}, u32[]{:S(2)}) collective-permute-start(bf16[80,1152]{1,0:T(8,128)(2,1)} %pad_maximum_fusion.1), channel_id=1, source_target_pairs={{0,8},{4,12},{8,0},{12,4},{1,9},{5,13},{9,1},{13,5},{2,10},{6,14},... | collective-permute-start | bytes 552968 | tf_op jit(solution)/shard_map/ppermute | solution.py:18
  15.1 3.4 %collective-permute-start.2 = (bf16[128,1152]{1,0:T(8,128)(2,1)S(1)}, bf16[128,1152]{1,0:T(8,128)(2,1)}, u32[]{:S(2)}, u32[]{:S(2)}) collective-permute-start(bf16[128,1152]{1,0:T(8,128)(2,1)S(1)} %collective-permute-done.1.far), channel_id=1, source_target_pairs={{0,1},{1,0},{2,3},{3,2},{4,5},{5,4},{6,7},{7,6},{8,9},{9,8},{10,11... | collective-permute-start | bytes 884744 | tf_op jit(solution)/shard_map/ppermute | solution.py:23
  15.8 19.5 %collective-permute-start.9 = (bf16[80,1152]{1,0:T(8,128)(2,1)}, bf16[80,1152]{1,0:T(8,128)(2,1)S(1)}, u32[]{:S(2)}, u32[]{:S(2)}) collective-permute-start(bf16[80,1152]{1,0:T(8,128)(2,1)} %pad_maximum_fusion), channel_id=1, source_target_pairs={{0,4},{4,8},{8,12},{12,0},{1,5},{5,9},{9,13},{13,1},{2,6},{6,10},{... | collective-permute-start | bytes 552968 | tf_op jit(solution)/shard_map/ppermute | solution.py:18
  21.1 11.2 %copy-start.24 = (bf16[16,1152]{1,0:T(8,128)(2,1)S(1)}, bf16[16,1152]{1,0:T(8,128)(2,1)}, u32[]{:S(2)}) copy-start(bf16[16,1152]{1,0:T(8,128)(2,1)} %get-tuple-element.27) | copy-start | bytes 110596
  25.8 19.1 %collective-permute-start.6 = (bf16[656,256]{1,0:T(8,128)(2,1)S(1)}, bf16[656,256]{1,0:T(8,128)(2,1)}, u32[]{:S(2)}, u32[]{:S(2)}) collective-permute-start(bf16[656,256]{1,0:T(8,128)(2,1)S(1)} %shard_map.82.refs_0_), channel_id=1, source_target_pairs={{12,8},{8,4},{4,0},{13,9},{9,5},{5,1},{14,10},{10,6},{6,2},{15,11}... | collective-permute-start | bytes 1007624 | tf_op jit(solution)/shard_map/ppermute | solution.py:256
  27.1 19.1 %collective-permute-start.3 = (bf16[656,256]{1,0:T(8,128)(2,1)S(1)}, bf16[656,256]{1,0:T(8,128)(2,1)}, u32[]{:S(2)}, u32[]{:S(2)}) collective-permute-start(bf16[656,256]{1,0:T(8,128)(2,1)S(1)} %shard_map.82.refs_0_), channel_id=1, source_target_pairs={{0,4},{4,8},{8,12},{1,5},{5,9},{9,13},{2,6},{6,10},{10,14},{3,7},{... | collective-permute-start | bytes 1007624 | tf_op jit(solution)/shard_map/ppermute | solution.py:255
  32.4 10.4 %collective-permute-start.11 = (bf16[80,1152]{1,0:T(8,128)(2,1)S(1)}, bf16[80,1152]{1,0:T(8,128)(2,1)S(1)}, u32[]{:S(2)}, u32[]{:S(2)}) collective-permute-start(bf16[80,1152]{1,0:T(8,128)(2,1)S(1)} %pad_maximum_fusion.2), channel_id=1, source_target_pairs={{0,12},{4,0},{8,4},{12,8},{1,13},{5,1},{9,5},{13,9},{2,14},{6,2},{... | collective-permute-start | bytes 552968 | tf_op jit(solution)/shard_map/ppermute | solution.py:18
  33.8 10.5 %collective-permute-start.16 = (bf16[80,1152]{1,0:T(8,128)(2,1)S(1)}, bf16[80,1152]{1,0:T(8,128)(2,1)}, u32[]{:S(2)}, u32[]{:S(2)}) collective-permute-start(bf16[80,1152]{1,0:T(8,128)(2,1)S(1)} %collective-permute-done.10.third.own), channel_id=1, source_target_pairs={{0,2},{1,3},{2,0},{3,1},{4,6},{5,7},{6,4},{7,5},{8,10},{9,11},{10,... | collective-permute-start | bytes 552968 | tf_op jit(solution)/shard_map/ppermute | solution.py:23
  35.3 12.8 %collective-permute-start.15 = (bf16[80,1152]{1,0:T(8,128)(2,1)S(1)}, bf16[80,1152]{1,0:T(8,128)(2,1)}, u32[]{:S(2)}, u32[]{:S(2)}) collective-permute-start(bf16[80,1152]{1,0:T(8,128)(2,1)S(1)} %collective-permute-done.10.third.own), channel_id=1, source_target_pairs={{0,1},{1,0},{2,3},{3,2},{4,5},{5,4},{6,7},{7,6},{8,9},{9,8},{10,11... | collective-permute-start | bytes 552968 | tf_op jit(solution)/shard_map/ppermute | solution.py:23
  42.8 7.6 %collective-permute-start.19 = (bf16[80,1152]{1,0:T(8,128)(2,1)S(1)}, bf16[80,1152]{1,0:T(8,128)(2,1)}, u32[]{:S(2)}, u32[]{:S(2)}) collective-permute-start(bf16[80,1152]{1,0:T(8,128)(2,1)S(1)} %collective-permute-done.11.fourth.own), channel_id=1, source_target_pairs={{0,2},{1,3},{2,0},{3,1},{4,6},{5,7},{6,4},{7,5},{8,10},{9,11},{10,... | collective-permute-start | bytes 552968 | tf_op jit(solution)/shard_map/ppermute | solution.py:23
  44.3 8.1 %collective-permute-start.13 = (bf16[80,1152]{1,0:T(8,128)(2,1)S(1)}, bf16[80,1152]{1,0:T(8,128)(2,1)S(1)}, u32[]{:S(2)}, u32[]{:S(2)}) collective-permute-start(bf16[80,1152]{1,0:T(8,128)(2,1)S(1)} %collective-permute-done.9.second.own), channel_id=1, source_target_pairs={{0,2},{1,3},{2,0},{3,1},{4,6},{5,7},{6,4},{7,5},{8,10},{9,11},{10,... | collective-permute-start | bytes 552968 | tf_op jit(solution)/shard_map/ppermute | solution.py:23
  44.9 10.5 %collective-permute-start.7 = (bf16[656,256]{1,0:T(8,128)(2,1)}, bf16[656,256]{1,0:T(8,128)(2,1)}, u32[]{:S(2)}, u32[]{:S(2)}) collective-permute-start(bf16[656,256]{1,0:T(8,128)(2,1)} %collective-permute-done.6.refs_4_), channel_id=1, source_target_pairs={{8,4},{4,0},{9,5},{5,1},{10,6},{6,2},{11,7},{7,3},{24,20},{20,16},... | collective-permute-start | bytes 1007624 | tf_op jit(solution)/shard_map/ppermute | solution.py:256
  46.2 10.5 %collective-permute-start.4 = (bf16[656,256]{1,0:T(8,128)(2,1)}, bf16[656,256]{1,0:T(8,128)(2,1)}, u32[]{:S(2)}, u32[]{:S(2)}) collective-permute-start(bf16[656,256]{1,0:T(8,128)(2,1)} %collective-permute-done.3.refs_1_), channel_id=1, source_target_pairs={{4,8},{8,12},{5,9},{9,13},{6,10},{10,14},{7,11},{11,15},{20,24},{2... | collective-permute-start | bytes 1007624 | tf_op jit(solution)/shard_map/ppermute | solution.py:255
  48.1 5.5 %collective-permute-start.18 = (bf16[80,1152]{1,0:T(8,128)(2,1)S(1)}, bf16[80,1152]{1,0:T(8,128)(2,1)}, u32[]{:S(2)}, u32[]{:S(2)}) collective-permute-start(bf16[80,1152]{1,0:T(8,128)(2,1)S(1)} %collective-permute-done.11.fourth.own), channel_id=1, source_target_pairs={{0,1},{1,0},{2,3},{3,2},{4,5},{5,4},{6,7},{7,6},{8,9},{9,8},{10,11... | collective-permute-start | bytes 552968 | tf_op jit(solution)/shard_map/ppermute | solution.py:23
  50.4 3.7 %collective-permute-start.20 = (bf16[80,1152]{1,0:T(8,128)(2,1)}, bf16[80,1152]{1,0:T(8,128)(2,1)}, u32[]{:S(2)}, u32[]{:S(2)}) collective-permute-start(bf16[80,1152]{1,0:T(8,128)(2,1)} %collective-permute-done.19.far), channel_id=1, source_target_pairs={{0,1},{1,0},{2,3},{3,2},{4,5},{5,4},{6,7},{7,6},{8,9},{9,8},{10,11... | collective-permute-start | bytes 552968 | tf_op jit(solution)/shard_map/ppermute | solution.py:23
  53.0 9.2 %collective-permute-start.17 = (bf16[80,1152]{1,0:T(8,128)(2,1)}, bf16[80,1152]{1,0:T(8,128)(2,1)}, u32[]{:S(2)}, u32[]{:S(2)}) collective-permute-start(bf16[80,1152]{1,0:T(8,128)(2,1)} %collective-permute-done.16.far), channel_id=1, source_target_pairs={{0,1},{1,0},{2,3},{3,2},{4,5},{5,4},{6,7},{7,6},{8,9},{9,8},{10,11... | collective-permute-start | bytes 552968 | tf_op jit(solution)/shard_map/ppermute | solution.py:23
  53.7 11.2 %collective-permute-start.12 = (bf16[80,1152]{1,0:T(8,128)(2,1)S(1)}, bf16[80,1152]{1,0:T(8,128)(2,1)}, u32[]{:S(2)}, u32[]{:S(2)}) collective-permute-start(bf16[80,1152]{1,0:T(8,128)(2,1)S(1)} %collective-permute-done.9.second.own), channel_id=1, source_target_pairs={{0,1},{1,0},{2,3},{3,2},{4,5},{5,4},{6,7},{7,6},{8,9},{9,8},{10,11... | collective-permute-start | bytes 552968 | tf_op jit(solution)/shard_map/ppermute | solution.py:23
  54.2 10.7 %collective-permute-start.14 = (bf16[80,1152]{1,0:T(8,128)(2,1)}, bf16[80,1152]{1,0:T(8,128)(2,1)}, u32[]{:S(2)}, u32[]{:S(2)}) collective-permute-start(bf16[80,1152]{1,0:T(8,128)(2,1)} %copy-done.21), channel_id=1, source_target_pairs={{0,1},{1,0},{2,3},{3,2},{4,5},{5,4},{6,7},{7,6},{8,9},{9,8},{10,11... | collective-permute-start | bytes 552968 | tf_op jit(solution)/shard_map/ppermute | solution.py:23
  55.3 14.8 %collective-permute-start.8 = (bf16[656,256]{1,0:T(8,128)(2,1)}, bf16[656,256]{1,0:T(8,128)(2,1)}, u32[]{:S(2)}, u32[]{:S(2)}) collective-permute-start(bf16[656,256]{1,0:T(8,128)(2,1)} %collective-permute-done.7.refs_5_), channel_id=1, source_target_pairs={{4,0},{5,1},{6,2},{7,3},{20,16},{21,17},{22,18},{23,19}} | collective-permute-start | bytes 1007624 | tf_op jit(solution)/shard_map/ppermute | solution.py:256
  56.6 13.5 %collective-permute-start.5 = (bf16[656,256]{1,0:T(8,128)(2,1)}, bf16[656,256]{1,0:T(8,128)(2,1)}, u32[]{:S(2)}, u32[]{:S(2)}) collective-permute-start(bf16[656,256]{1,0:T(8,128)(2,1)} %collective-permute-done.4.refs_2_), channel_id=1, source_target_pairs={{8,12},{9,13},{10,14},{11,15},{24,28},{25,29},{26,30},{27,31}} | collective-permute-start | bytes 1007624 | tf_op jit(solution)/shard_map/ppermute | solution.py:255
  62.2 8.0 %copy-start.1 = (bf16[256,1024]{1,0:T(8,128)(2,1)}, bf16[256,1024]{1,0:T(8,128)(2,1)S(1)}, u32[]{:S(2)}) copy-start(bf16[256,1024]{1,0:T(8,128)(2,1)S(1)} %get-tuple-element.16.refs_10_) | copy-start | bytes 1572868
  62.2 8.0 %copy-start.12 = (f32[256,256]{1,0:T(8,128)}, f32[256,256]{1,0:T(8,128)S(1)}, u32[]{:S(2)}) copy-start(f32[256,256]{1,0:T(8,128)S(1)} %get-tuple-element.20.refs_14_) | copy-start | bytes 786436
  64.9 9.0 %copy-start.3 = (bf16[256,1024]{1,0:T(8,128)(2,1)}, bf16[256,1024]{1,0:T(8,128)(2,1)S(1)}, u32[]{:S(2)}) copy-start(bf16[256,1024]{1,0:T(8,128)(2,1)S(1)} %get-tuple-element.15.refs_9_) | copy-start | bytes 1572868
  64.9 9.0 %copy-start.14 = (f32[256,256]{1,0:T(8,128)}, f32[256,256]{1,0:T(8,128)S(1)}, u32[]{:S(2)}) copy-start(f32[256,256]{1,0:T(8,128)S(1)} %get-tuple-element.19.refs_13_) | copy-start | bytes 786436
  73.9 11.9 %collective-permute-start.21 = (f32[128,1024]{1,0:T(8,128)S(1)}, f32[128,1024]{1,0:T(8,128)}, u32[]{:S(2)}, u32[]{:S(2)}) collective-permute-start(f32[128,1024]{1,0:T(8,128)S(1)} %shard_map.88), channel_id=1, source_target_pairs={{0,1},{1,0},{2,3},{3,2},{4,5},{5,4},{6,7},{7,6},{8,9},{9,8},{10,11... | collective-permute-start | bytes 1572872 | tf_op jit(solution)/shard_map/ppermute | solution.py:23
  86.8 6.0 %collective-permute-start.22 = (bf16[64,1024]{1,0:T(8,128)(2,1)S(1)}, bf16[64,1024]{1,0:T(8,128)(2,1)S(1)}, u32[]{:S(2)}, u32[]{:S(2)}) collective-permute-start(bf16[64,1024]{1,0:T(8,128)(2,1)S(1)} %fusion), channel_id=1, source_target_pairs={{0,2},{1,3},{2,0},{3,1},{4,6},{5,7},{6,4},{7,5},{8,10},{9,11},{10,... | collective-permute-start | bytes 393224 | tf_op jit(solution)/shard_map/ppermute | solution.py:23
  93.7 10.2 %collective-permute-start.23 = (bf16[64,256]{1,0:T(8,128)(2,1)S(1)}, bf16[64,256]{1,0:T(8,128)(2,1)S(1)}, u32[]{:S(2)}, u32[]{:S(2)}) collective-permute-start(bf16[64,256]{1,0:T(8,128)(2,1)S(1)} %get-tuple-element.31), channel_id=1, source_target_pairs={{0,12},{4,0},{8,4},{12,8},{1,13},{5,1},{9,5},{13,9},{2,14},{6,2},{... | collective-permute-start | bytes 98312 | tf_op jit(solution)/shard_map/ppermute | solution.py:18
  98.1 6.0 %collective-permute-start.25 = (bf16[64,256]{1,0:T(8,128)(2,1)S(1)}, bf16[64,256]{1,0:T(8,128)(2,1)S(1)}, u32[]{:S(2)}, u32[]{:S(2)}) collective-permute-start(bf16[64,256]{1,0:T(8,128)(2,1)S(1)} %get-tuple-element.32), channel_id=1, source_target_pairs={{0,4},{4,8},{8,12},{12,0},{1,5},{5,9},{9,13},{13,1},{2,6},{6,10},{... | collective-permute-start | bytes 98312 | tf_op jit(solution)/shard_map/ppermute | solution.py:18
  98.1 6.2 %collective-permute-start.24 = (bf16[64,256]{1,0:T(8,128)(2,1)S(1)}, bf16[64,256]{1,0:T(8,128)(2,1)S(1)}, u32[]{:S(2)}, u32[]{:S(2)}) collective-permute-start(bf16[64,256]{1,0:T(8,128)(2,1)S(1)} %get-tuple-element.33), channel_id=1, source_target_pairs={{0,8},{4,12},{8,0},{12,4},{1,9},{5,13},{9,1},{13,5},{2,10},{6,14},... | collective-permute-start | bytes 98312 | tf_op jit(solution)/shard_map/ppermute | solution.py:18
  (22 other events, 57.7 us)
